TPU v7x, 512 devices: a whole 4x8x8 slice. The times are simulated.
512 devices in a mesh: dp: 8 (over y_hi, core), expert: 64 (over z, x, y_lo).
Axes of the slice: x: 4, y: 8 (y_hi: 4, y_lo: 2; y = y_hi * 2 + y_lo), z: 8, core: 2. Of those that a mesh axis runs over, the one named last changes fastest.
Arguments:
- tokens: bfloat16 [65536, 3584], P(('dp', 'expert')), may hold values from -6 to 6
- cotangent: bfloat16 [65536, 3584], P(('dp', 'expert')), may hold values from -0.59765625 to 0.59765625
- route_ids: int32 [65536, 8], P(('dp', 'expert')), may hold values from 0 to 383, as said below
- gates: bfloat16 [65536, 8], P(('dp', 'expert')), may hold values from 0.099609375 to 1
- w_gate: bfloat16 [64, 3584, 128], P('expert', None, 'dp'), may hold values from -0.09375 to 0.09375
- w_up: bfloat16 [64, 3584, 128], P('expert', None, 'dp'), may hold values from -0.09375 to 0.09375
- w_down: bfloat16 [64, 3584, 128], P('expert', None, 'dp'), may hold values from -0.125 to 0.125
Outputs:
- relaid_gate: bfloat16 [64, 3584, 128], P('expert', 'dp')
- relaid_up: bfloat16 [64, 3584, 128], P('expert', 'dp')
- relaid_down: bfloat16 [64, 3584, 128], P('expert', 'dp')
- grad_gate: float32 [64, 3584, 128], P('expert', 'dp')
- grad_up: float32 [64, 3584, 128], P('expert', 'dp')
- grad_down: float32 [64, 3584, 128], P('expert', 'dp')
- token_grad: bfloat16 [65536, 3584], P(('dp', 'expert'))
- gate_grad: float32 [65536, 8], P(('dp', 'expert'))
Inputs may be any that keep to these rules, and one draw needn't show every extreme that they name: `route_ids`: each row names 8 different experts. Among the 128 rows of one device, at most 6 routes name any one expert below 4; on every device of one index of dp, one same expert below 4 is named by exactly 6 routes.
All inputs are finite; a program needn't handle non-finite values.
Results may differ from a plain program's by a relative error of at most 0.02.
Values may be sent and summed in bfloat16 or wider, within the bound.
No kernel may reach another device: no remote copies, remote signals or barrier semaphores. Data moves between devices by JAX's collectives and lax.ppermute only.
A program may use at most 128 MiB of HBM per device.

v0:
```python
import jax
import jax.numpy as jnp
from jax import lax
from jax.sharding import PartitionSpec as P

HSPLIT = 16
CAP = 6


def copies(values, experts):
    grouped = values.reshape((experts, CAP) + values.shape[1:])
    return jnp.repeat(grouped, HSPLIT, axis=0)


def forward_part(slot_tokens, gate_slab, up_slab):
    pre_gate = jnp.dot(slot_tokens, gate_slab, preferred_element_type=jnp.float32)
    pre_up = jnp.dot(slot_tokens, up_slab, preferred_element_type=jnp.float32)
    sigmoid_gate = jax.nn.sigmoid(pre_gate)
    activation = pre_gate * sigmoid_gate
    hidden = (activation * pre_up).astype(jnp.bfloat16)
    return (pre_gate, pre_up, sigmoid_gate, activation, hidden)


def shards(tokens, cotangent, route_ids, gates, w_gate, w_up, w_down):
    slabs = lax.axis_size("expert")
    experts = slabs // HSPLIT
    tok_count, features = tokens.shape
    top_count = route_ids.shape[1]
    slot_total = experts * CAP
    flat_ids = route_ids.reshape(-1)
    expert_hits = (flat_ids[:, None] == jnp.arange(experts, dtype=jnp.int32)[None, :]).astype(
        jnp.int32
    )
    earlier = jnp.cumsum(expert_hits, axis=0) - expert_hits
    slot_rank = jnp.sum(earlier * expert_hits, axis=1)
    in_slab = jnp.sum(expert_hits, axis=1) > 0
    slot_index = flat_ids * CAP + slot_rank
    table = (slot_index[:, None] == jnp.arange(slot_total, dtype=jnp.int32)[None, :]) & in_slab[
        :, None
    ]
    select = table.reshape(tok_count, top_count, slot_total)
    picked = jnp.any(select, axis=1)
    pick_half = picked.astype(jnp.bfloat16)
    token_slots = jnp.einsum(
        "tc,td->cd", pick_half, tokens, preferred_element_type=jnp.float32
    ).astype(jnp.bfloat16)
    cotan_slots = jnp.einsum(
        "tc,td->cd", pick_half, cotangent, preferred_element_type=jnp.float32
    ).astype(jnp.bfloat16)
    gate_slots = jnp.sum(
        jnp.where(select, gates[:, :, None].astype(jnp.float32), 0.0), axis=(0, 1)
    ).astype(jnp.bfloat16)
    send_tok = copies(token_slots, experts)
    send_cotan = copies(cotan_slots, experts)
    send_gate = copies(gate_slots, experts)
    new_gate, new_up, new_down = (
        lax.all_to_all(w_gate, "dp", split_axis=1, concat_axis=2, tiled=True),
        lax.all_to_all(w_up, "dp", split_axis=1, concat_axis=2, tiled=True),
        lax.all_to_all(w_down, "dp", split_axis=1, concat_axis=2, tiled=True),
    )
    full_gate, full_up, full_down = (
        lax.all_gather(new_gate, "dp", axis=1, tiled=True),
        lax.all_gather(new_up, "dp", axis=1, tiled=True),
        lax.all_gather(new_down, "dp", axis=1, tiled=True),
    )
    gate_slab = full_gate[0]
    up_slab = full_up[0]
    down_slab = full_down[0]
    recv_tok, recv_cotan, recv_gate = (
        lax.all_to_all(send_tok, "expert", split_axis=0, concat_axis=0, tiled=True),
        lax.all_to_all(send_cotan, "expert", split_axis=0, concat_axis=0, tiled=True),
        lax.all_to_all(send_gate, "expert", split_axis=0, concat_axis=0, tiled=True),
    )
    slot_tokens = recv_tok.reshape(-1, features)
    pre_gate, pre_up, sigmoid_gate, activation, hidden = forward_part(
        slot_tokens, gate_slab, up_slab
    )
    slot_cotan = recv_cotan.reshape(-1, features)
    slot_gates = recv_gate.reshape(-1).astype(jnp.float32)[:, None]
    back_proj = jnp.dot(slot_cotan, down_slab, preferred_element_type=jnp.float32)
    score_part = jnp.sum(hidden.astype(jnp.float32) * back_proj, axis=1).astype(jnp.bfloat16)
    scaled = slot_gates * back_proj
    d_gate = (scaled * pre_up * sigmoid_gate * (1.0 + pre_gate * (1.0 - sigmoid_gate))).astype(
        jnp.bfloat16
    )
    d_up = (scaled * activation).astype(jnp.bfloat16)
    hidden_gated = (slot_gates * hidden.astype(jnp.float32)).astype(jnp.bfloat16)
    partial_value = (
        jnp.einsum("rh,dh->rd", d_gate, gate_slab, preferred_element_type=jnp.float32)
        + jnp.einsum("rh,dh->rd", d_up, up_slab, preferred_element_type=jnp.float32)
    ).astype(jnp.bfloat16)
    grad_gate_part = jnp.einsum(
        "rd,rh->dh", slot_tokens, d_gate, preferred_element_type=jnp.float32
    )
    grad_up_part = jnp.einsum("rd,rh->dh", slot_tokens, d_up, preferred_element_type=jnp.float32)
    grad_down_part = jnp.einsum(
        "rd,rh->dh", slot_cotan, hidden_gated, preferred_element_type=jnp.float32
    )
    grad_gate, grad_up, grad_down = (
        lax.psum_scatter(
            grad_gate_part[None].astype(jnp.bfloat16), "dp", scatter_dimension=1, tiled=True
        ).astype(jnp.float32),
        lax.psum_scatter(
            grad_up_part[None].astype(jnp.bfloat16), "dp", scatter_dimension=1, tiled=True
        ).astype(jnp.float32),
        lax.psum_scatter(
            grad_down_part[None].astype(jnp.bfloat16), "dp", scatter_dimension=1, tiled=True
        ).astype(jnp.float32),
    )
    back_parts, back_scores = (
        lax.all_to_all(
            partial_value.reshape(slabs, CAP, features),
            "expert",
            split_axis=0,
            concat_axis=0,
            tiled=True,
        ),
        lax.all_to_all(
            score_part.reshape(slabs, CAP), "expert", split_axis=0, concat_axis=0, tiled=True
        ),
    )
    part_sum = jnp.sum(
        back_parts.reshape(experts, HSPLIT, CAP, features).astype(jnp.float32), axis=1
    )
    part_sum = part_sum.reshape(slot_total, features)
    score_sum = jnp.sum(
        back_scores.reshape(experts, HSPLIT, CAP).astype(jnp.float32), axis=1
    ).reshape(slot_total)
    token_grad = jnp.einsum(
        "tc,cd->td", picked.astype(jnp.float32), part_sum, precision=lax.Precision.HIGHEST
    ).astype(jnp.bfloat16)
    gate_grad = jnp.einsum(
        "tkc,c->tk", select.astype(jnp.float32), score_sum, precision=lax.Precision.HIGHEST
    )
    return (new_gate, new_up, new_down, grad_gate, grad_up, grad_down, token_grad, gate_grad)


def solution(mesh):
    in_specs = (
        P(("dp", "expert"), None),
        P(("dp", "expert"), None),
        P(("dp", "expert"), None),
        P(("dp", "expert"), None),
        P("expert", None, "dp"),
        P("expert", None, "dp"),
        P("expert", None, "dp"),
    )
    out_specs = (
        P("expert", "dp", None),
        P("expert", "dp", None),
        P("expert", "dp", None),
        P("expert", "dp", None),
        P("expert", "dp", None),
        P("expert", "dp", None),
        P(("dp", "expert"), None),
        P(("dp", "expert"), None),
    )
    return jax.shard_map(shards, mesh=mesh, in_specs=in_specs, out_specs=out_specs, check_vma=False)
```

profile of v0, /device:TPU:17, one launch (start us, length us, event | category | flops | bytes accessed | tf_op | source)
XLA Modules:
  0.0 506.8 jit_solution(7459007044376049819)
XLA Ops:
  12.9 14.5 %all-to-all-start.4 = ((bf16[64,1,6]{2,1,0:T(2,128)(2,1)}), bf16[64,1,6]{2,1,0:T(2,128)(2,1)S(1)}, u32[]{:S(2)}, u32[]{:S(2)}) async-start(bf16[64,1,6]{2,1,0:T(2,128)(2,1)} %copy.119), calls=%async_computation.4 | async-start | bytes 65536 | tf_op jit(solution)/shard_map/all_to_all | solution.py:72
  27.4 3.7 copy.105
  31.7 20.6 %reduce.6 = bf16[3584,16]{1,0:T(8,128)(2,1)} reduce(bf16[3584,1,16]{2,1,0:T(2,128)(2,1)S(1)} %bitcast.87, bf16[]{:T(256)} %broadcast.78), dimensions={1}, to_apply=%bitcast.58.reduce_sub_computation | reduce | bytes 229378
  55.1 7.4 %all-to-all-start = ((bf16[8,2,3584]{2,1,0:T(2,128)(2,1)}), bf16[8,2,3584]{2,1,0:T(2,128)(2,1)S(1)}, u32[]{:S(2)}, u32[]{:S(2)}) async-start(bf16[8,2,3584]{2,1,0:T(2,128)(2,1)} %reshape.176), calls=%async_computation | async-start | bytes 229376 | tf_op jit(solution)/shard_map/all_to_all | solution.py:57
  65.0 20.6 %reduce.7 = bf16[3584,16]{1,0:T(8,128)(2,1)} reduce(bf16[3584,1,16]{2,1,0:T(2,128)(2,1)S(1)} %bitcast.92, bf16[]{:T(256)} %broadcast.78), dimensions={1}, to_apply=%bitcast.60.reduce_sub_computation | reduce | bytes 229378
  88.4 7.8 %all-to-all-start.1 = ((bf16[8,2,3584]{2,1,0:T(2,128)(2,1)}), bf16[8,2,3584]{2,1,0:T(2,128)(2,1)S(1)}, u32[]{:S(2)}, u32[]{:S(2)}) async-start(bf16[8,2,3584]{2,1,0:T(2,128)(2,1)} %reshape.178), calls=%async_computation.1 | async-start | bytes 229376 | tf_op jit(solution)/shard_map/all_to_all | solution.py:58
  98.7 20.6 %reduce.8 = bf16[3584,16]{1,0:T(8,128)(2,1)} reduce(bf16[3584,1,16]{2,1,0:T(2,128)(2,1)S(1)} %bitcast.88, bf16[]{:T(256)} %broadcast.78), dimensions={1}, to_apply=%bitcast.62.reduce_sub_computation | reduce | bytes 229378
  122.1 7.2 %all-to-all-start.2 = ((bf16[8,2,3584]{2,1,0:T(2,128)(2,1)}), bf16[8,2,3584]{2,1,0:T(2,128)(2,1)S(1)}, u32[]{:S(2)}, u32[]{:S(2)}) async-start(bf16[8,2,3584]{2,1,0:T(2,128)(2,1)} %reshape.180), calls=%async_computation.2 | async-start | bytes 229376 | tf_op jit(solution)/shard_map/all_to_all | solution.py:59
  129.6 5.3 %all-to-all-done.2 = bf16[8,2,3584]{2,1,0:T(2,128)(2,1)S(1)} async-done(((bf16[8,2,3584]{2,1,0:T(2,128)(2,1)}), bf16[8,2,3584]{2,1,0:T(2,128)(2,1)S(1)}, u32[]{:S(2)}, u32[]{:S(2)}) %all-to-all-start.2) | async-done | bytes 114720 | tf_op jit(solution)/shard_map/all_to_all | solution.py:59
  137.0 11.7 %all-to-all-start.3 = ((bf16[64,6,3584]{2,1,0:T(8,128)(2,1)}), bf16[64,6,3584]{2,1,0:T(8,128)(2,1)}, u32[]{:S(2)}, u32[]{:S(2)}) async-start(bf16[64,6,3584]{2,1,0:T(8,128)(2,1)} %bitcast.86), calls=%async_computation.3 | async-start | bytes 7340032 | tf_op jit(solution)/shard_map/all_to_all | solution.py:70
  149.0 82.7 %all-to-all-done.3 = bf16[64,6,3584]{2,1,0:T(8,128)(2,1)} async-done(((bf16[64,6,3584]{2,1,0:T(8,128)(2,1)}), bf16[64,6,3584]{2,1,0:T(8,128)(2,1)}, u32[]{:S(2)}, u32[]{:S(2)}) %all-to-all-start.3) | async-done | bytes 2752544 | tf_op jit(solution)/shard_map/all_to_all | solution.py:70
  233.9 8.0 %all-to-all-start.5 = ((bf16[64,6,3584]{2,1,0:T(8,128)(2,1)}), bf16[64,6,3584]{2,1,0:T(8,128)(2,1)}, u32[]{:S(2)}, u32[]{:S(2)}) async-start(bf16[64,6,3584]{2,1,0:T(8,128)(2,1)} %bitcast.85), calls=%async_computation.5 | async-start | bytes 7340032 | tf_op jit(solution)/shard_map/all_to_all | solution.py:71
  252.9 47.2 %all_gather.10 = bf16[1,3584,128]{2,1,0:T(8,128)(2,1)S(1)} all-gather(bf16[1,448,128]{2,1,0:T(8,128)(2,1)S(1)} %copy.126), channel_id=1, replica_groups=mesh['dp'=8,'expert'=64] {'dp'}, dimensions={1}, use_global_device_ids=true | all-gather | bytes 1032192 | tf_op jit(solution)/shard_map/all_gather | solution.py:63
  300.0 16.3 %all_gather.11 = bf16[1,3584,128]{2,1,0:T(8,128)(2,1)S(1)} all-gather(bf16[1,448,128]{2,1,0:T(8,128)(2,1)S(1)} %copy.125), channel_id=1, replica_groups=mesh['dp'=8,'expert'=64] {'dp'}, dimensions={1}, use_global_device_ids=true | all-gather | bytes 1032192 | tf_op jit(solution)/shard_map/all_gather | solution.py:62
  316.4 16.9 %all_gather.9 = bf16[1,3584,128]{2,1,0:T(8,128)(2,1)} all-gather(bf16[1,448,128]{2,1,0:T(8,128)(2,1)S(1)} %copy.127), channel_id=1, replica_groups=mesh['dp'=8,'expert'=64] {'dp'}, dimensions={1}, use_global_device_ids=true | all-gather | bytes 1032192 | tf_op jit(solution)/shard_map/all_gather | solution.py:64
  333.3 5.5 %reshape.155 = bf16[384,3584]{1,0:T(8,128)(2,1)} reshape(bf16[64,6,3584]{2,1,0:T(8,128)(2,1)} %all-to-all-done.3) | data formatting | bytes 5505024 | tf_op jit(solution)/shard_map/reshape | solution.py:74
  342.6 5.5 %reshape.158 = bf16[384,3584]{1,0:T(8,128)(2,1)} reshape(bf16[64,6,3584]{2,1,0:T(8,128)(2,1)} %all-to-all-done.5) | data formatting | bytes 5505024 | tf_op jit(solution)/shard_map/reshape | solution.py:78
  357.2 16.3 %all-to-all-start.7 = ((bf16[64,1,6]{2,1,0:T(2,128)(2,1)}), bf16[64,1,6]{2,1,0:T(2,128)(2,1)S(1)}, u32[]{:S(2)}, u32[]{:S(2)}) async-start(bf16[64,1,6]{2,1,0:T(2,128)(2,1)} %convert_element_type.149), calls=%async_computation.10 | async-start | bytes 65536 | tf_op jit(solution)/shard_map/all_to_all | solution.py:118
  373.4 5.1 fusion
  378.5 5.5 %reshape.159 = bf16[64,6,3584]{2,1,0:T(8,128)(2,1)} reshape(bf16[384,3584]{1,0:T(8,128)(2,1)} %fusion) | data formatting | bytes 5505024 | tf_op jit(solution)/shard_map/reshape | solution.py:112
  383.9 10.8 %all-to-all-start.6 = ((bf16[64,6,3584]{2,1,0:T(8,128)(2,1)}), bf16[64,6,3584]{2,1,0:T(8,128)(2,1)}, u32[]{:S(2)}, u32[]{:S(2)}) async-start(bf16[64,6,3584]{2,1,0:T(8,128)(2,1)} %reshape.159), calls=%async_computation.9 | async-start | bytes 7340032 | tf_op jit(solution)/shard_map/all_to_all | solution.py:111
  394.8 3.7 fusion.2
  405.5 44.8 %reduce-scatter.6.cloned.1.call-done = bf16[1,448,128]{2,1,0:T(8,128)(2,1)} async-done(((bf16[1,3584,128]{2,1,0:T(8,128)(2,1)}), bf16[1,448,128]{2,1,0:T(8,128)(2,1)}) %reduce-scatter.6.cloned.1.call-update) | async-done | bytes 114704 | tf_op jit(solution)/shard_map/reduce_scatter | solution.py:103
  451.9 41.8 %reduce-scatter.8.cloned.1.call-done = bf16[1,448,128]{2,1,0:T(8,128)(2,1)} async-done(((bf16[1,3584,128]{2,1,0:T(8,128)(2,1)}), bf16[1,448,128]{2,1,0:T(8,128)(2,1)}) %reduce-scatter.8.cloned.1.call-update) | async-done | bytes 114704 | tf_op jit(solution)/shard_map/reduce_scatter | solution.py:106
  (100 shorter events, 63.0 us)
Async XLA Ops:
  7.2 122.1 %copy-start = (bf16[128,3584]{1,0:T(8,128)(2,1)S(1)}, bf16[128,3584]{1,0:T(8,128)(2,1)}, u32[]{:S(2)}) copy-start(bf16[128,3584]{1,0:T(8,128)(2,1)} %param.7) | copy-start | bytes 2752516
  12.9 42.2 %all-to-all-start.4 = ((bf16[64,1,6]{2,1,0:T(2,128)(2,1)}), bf16[64,1,6]{2,1,0:T(2,128)(2,1)S(1)}, u32[]{:S(2)}, u32[]{:S(2)}) async-start(bf16[64,1,6]{2,1,0:T(2,128)(2,1)} %copy.119), calls=%async_computation.4 | async-start | bytes 65536 | tf_op jit(solution)/shard_map/all_to_all | solution.py:72
  27.4 35.1 %copy-start.7 = (bf16[1,3584,16]{1,2,0:T(8,128)(2,1)S(1)}, bf16[1,3584,16]{1,2,0:T(8,128)(2,1)}, u32[]{:S(2)}) copy-start(bf16[1,3584,16]{1,2,0:T(8,128)(2,1)} %param.12) | copy-start | bytes 344068
  55.1 33.3 %all-to-all-start = ((bf16[8,2,3584]{2,1,0:T(2,128)(2,1)}), bf16[8,2,3584]{2,1,0:T(2,128)(2,1)S(1)}, u32[]{:S(2)}, u32[]{:S(2)}) async-start(bf16[8,2,3584]{2,1,0:T(2,128)(2,1)} %reshape.176), calls=%async_computation | async-start | bytes 229376 | tf_op jit(solution)/shard_map/all_to_all | solution.py:57
  62.5 33.6 %copy-start.8 = (bf16[1,3584,16]{1,2,0:T(8,128)(2,1)S(1)}, bf16[1,3584,16]{1,2,0:T(8,128)(2,1)}, u32[]{:S(2)}) copy-start(bf16[1,3584,16]{1,2,0:T(8,128)(2,1)} %param.13) | copy-start | bytes 344068
  88.4 33.7 %all-to-all-start.1 = ((bf16[8,2,3584]{2,1,0:T(2,128)(2,1)}), bf16[8,2,3584]{2,1,0:T(2,128)(2,1)S(1)}, u32[]{:S(2)}, u32[]{:S(2)}) async-start(bf16[8,2,3584]{2,1,0:T(2,128)(2,1)} %reshape.178), calls=%async_computation.1 | async-start | bytes 229376 | tf_op jit(solution)/shard_map/all_to_all | solution.py:58
  122.1 12.8 %all-to-all-start.2 = ((bf16[8,2,3584]{2,1,0:T(2,128)(2,1)}), bf16[8,2,3584]{2,1,0:T(2,128)(2,1)S(1)}, u32[]{:S(2)}, u32[]{:S(2)}) async-start(bf16[8,2,3584]{2,1,0:T(2,128)(2,1)} %reshape.180), calls=%async_computation.2 | async-start | bytes 229376 | tf_op jit(solution)/shard_map/all_to_all | solution.py:59
  137.0 11.7 %copy-start.3 = (bf16[128,3584]{1,0:T(8,128)(2,1)S(1)}, bf16[128,3584]{1,0:T(8,128)(2,1)}, u32[]{:S(2)}) copy-start(bf16[128,3584]{1,0:T(8,128)(2,1)} %param.8) | copy-start | bytes 2752516
  137.0 94.7 %all-to-all-start.3 = ((bf16[64,6,3584]{2,1,0:T(8,128)(2,1)}), bf16[64,6,3584]{2,1,0:T(8,128)(2,1)}, u32[]{:S(2)}, u32[]{:S(2)}) async-start(bf16[64,6,3584]{2,1,0:T(8,128)(2,1)} %bitcast.86), calls=%async_computation.3 | async-start | bytes 7340032 | tf_op jit(solution)/shard_map/all_to_all | solution.py:70
  233.9 108.7 %all-to-all-start.5 = ((bf16[64,6,3584]{2,1,0:T(8,128)(2,1)}), bf16[64,6,3584]{2,1,0:T(8,128)(2,1)}, u32[]{:S(2)}, u32[]{:S(2)}) async-start(bf16[64,6,3584]{2,1,0:T(8,128)(2,1)} %bitcast.85), calls=%async_computation.5 | async-start | bytes 7340032 | tf_op jit(solution)/shard_map/all_to_all | solution.py:71
  241.9 162.1 %reduce-scatter.4.cloned.1.call-start = ((), (), s32[]{:S(2)}) async-start(), calls=%async_computation.11 | async-start | bytes 1032192 | tf_op jit(solution)/shard_map/reduce_scatter | solution.py:100
  245.7 54.3 %copy-start.4 = (bf16[1,448,128]{2,1,0:T(8,128)(2,1)}, bf16[1,448,128]{2,1,0:T(8,128)(2,1)S(1)}, u32[]{:S(2)}) copy-start(bf16[1,448,128]{2,1,0:T(8,128)(2,1)S(1)} %copy.125) | copy-start | bytes 344068
  249.3 50.8 %copy-start.5 = (bf16[1,448,128]{2,1,0:T(8,128)(2,1)}, bf16[1,448,128]{2,1,0:T(8,128)(2,1)S(1)}, u32[]{:S(2)}) copy-start(bf16[1,448,128]{2,1,0:T(8,128)(2,1)S(1)} %copy.126) | copy-start | bytes 344068
  252.9 85.9 %copy-start.6 = (bf16[1,448,128]{2,1,0:T(8,128)(2,1)}, bf16[1,448,128]{2,1,0:T(8,128)(2,1)S(1)}, u32[]{:S(2)}) copy-start(bf16[1,448,128]{2,1,0:T(8,128)(2,1)S(1)} %copy.127) | copy-start | bytes 344068
  338.8 2.9 copy-start.1
  348.1 3.1 copy-start.2
  357.2 26.8 %all-to-all-start.7 = ((bf16[64,1,6]{2,1,0:T(2,128)(2,1)}), bf16[64,1,6]{2,1,0:T(2,128)(2,1)S(1)}, u32[]{:S(2)}, u32[]{:S(2)}) async-start(bf16[64,1,6]{2,1,0:T(2,128)(2,1)} %convert_element_type.149), calls=%async_computation.10 | async-start | bytes 65536 | tf_op jit(solution)/shard_map/all_to_all | solution.py:118
  383.9 111.4 %all-to-all-start.6 = ((bf16[64,6,3584]{2,1,0:T(8,128)(2,1)}), bf16[64,6,3584]{2,1,0:T(8,128)(2,1)}, u32[]{:S(2)}, u32[]{:S(2)}) async-start(bf16[64,6,3584]{2,1,0:T(8,128)(2,1)} %reshape.159), calls=%async_computation.9 | async-start | bytes 7340032 | tf_op jit(solution)/shard_map/all_to_all | solution.py:111
  394.7 55.5 %reduce-scatter.6.cloned.1.call-start = ((), (), s32[]{:S(2)}) async-start(), calls=%async_computation.12 | async-start | bytes 1032192 | tf_op jit(solution)/shard_map/reduce_scatter | solution.py:103
  398.5 95.2 %reduce-scatter.8.cloned.1.call-start = ((), (), s32[]{:S(2)}) async-start(), calls=%async_computation.13 | async-start | bytes 1032192 | tf_op jit(solution)/shard_map/reduce_scatter | solution.py:106
Sparse Core Ops, SparseCore 0:
  356.5 47.3 reduce-scatter.3
  407.0 43.2 reduce-scatter.5
  453.1 40.5 reduce-scatter.7
where the time goes:
time: 514 us; the launch traced here: 507 us
  waiting for transfers between devices  175 us (34%)
  starting transfers between devices  84 us (16%)
  blocking collectives  80.4 us (16%)
  other arithmetic  72.6 us (14%)
  local copies, waits for them, and re-layouts  52.7 us (10%)
  matrix products  27.4 us (5%)
  between operations  14.4 us (3%)
    all_to_all x1, waiting for transfers between devices, shards(): lax.all_to_all(send_tok, 'expert', split_axis=0, concat_axis=0, tiled=True)  82.7 us
    unnamed x4, other arithmetic  61.9 us
    all_gather x1, blocking collectives, shards(): lax.all_gather(new_up, 'dp', axis=1, tiled=True)  47.2 us
    reduce_scatter x1, waiting for transfers between devices, shards(): lax.psum_scatter(grad_up_part[None].astype(jnp.bfloat16), 'dp', scatter_d...  44.8 us
    reduce_scatter x1, waiting for transfers between devices, shards(): lax.psum_scatter(grad_down_part[None].astype(jnp.bfloat16), 'dp', scatter...  41.8 us
    unnamed x32, local copies, waits for them, and re-layouts  23 us
    all_gather x1, blocking collectives, shards(): lax.all_gather(new_down, 'dp', axis=1, tiled=True)  16.9 us
    all_gather x1, blocking collectives, shards(): lax.all_gather(new_gate, 'dp', axis=1, tiled=True)  16.3 us
  transfers between devices with their start and end apart: 11, of which 5 were waited for; matrix products, arithmetic and copies ran while one was open for 24% of the time, Pallas kernels for 0%

commit v1 on v0

--- a/solution.py
+++ b/solution.py
@@ -61,7 +61,9 @@
     full_gate, full_up, full_down = (
         lax.all_gather(new_gate, "dp", axis=1, tiled=True),
         lax.all_gather(new_up, "dp", axis=1, tiled=True),
-        lax.all_gather(new_down, "dp", axis=1, tiled=True),
+        jnp.concatenate(
+            lax.all_to_all(jnp.stack([new_down] * lax.axis_size("dp")), "dp", 0, 0), axis=1
+        ),
     )
     gate_slab = full_gate[0]
     up_slab = full_up[0]

time: 514 us -> 561 us (1.091)
  the two profiles are of different devices: /device:TPU:17 before, /device:TPU:23 now
where the time goes in v1:
time: 561 us; the launch traced here: 553 us
  waiting for transfers between devices  254 us (45%)
  starting transfers between devices  84.3 us (15%)
  other arithmetic  72.6 us (13%)
  local copies, waits for them, and re-layouts  54.5 us (10%)
  blocking collectives  45.4 us (8%)
  matrix products  28 us (5%)
  between operations  14.4 us (3%)
    all_to_all x1, waiting for transfers between devices, shards(): lax.all_to_all(send_tok, 'expert', split_axis=0, concat_axis=0, tiled=True)  83.3 us
    all_to_all x1, waiting for transfers between devices, shards(): lax.all_to_all(send_cotan, 'expert', split_axis=0, concat_axis=0, tiled=T...  79.2 us
    unnamed x4, other arithmetic  61.9 us
    reduce_scatter x1, waiting for transfers between devices, shards(): lax.psum_scatter(grad_up_part[None].astype(jnp.bfloat16), 'dp', scatter_d...  44.4 us
    reduce_scatter x1, waiting for transfers between devices, shards(): lax.psum_scatter(grad_down_part[None].astype(jnp.bfloat16), 'dp', scatter...  41.5 us
    all_gather x1, blocking collectives, shards(): lax.all_gather(new_up, 'dp', axis=1, tiled=True)  28.9 us
    unnamed x32, local copies, waits for them, and re-layouts  23.6 us
    all_gather x1, blocking collectives, shards(): lax.all_gather(new_gate, 'dp', axis=1, tiled=True)  16.6 us
  transfers between devices with their start and end apart: 12, of which 5 were waited for; matrix products, arithmetic and copies ran while one was open for 24% of the time, Pallas kernels for 0%

profile of v1, /device:TPU:23, one launch (start us, length us, event | category | flops | bytes accessed | tf_op | source)
XLA Modules:
  0.0 553.0 jit_solution(3049701806953665745)
XLA Ops:
  12.9 14.3 %all-to-all-start.4 = ((bf16[64,1,6]{2,1,0:T(2,128)(2,1)}), bf16[64,1,6]{2,1,0:T(2,128)(2,1)S(1)}, u32[]{:S(2)}, u32[]{:S(2)}) async-start(bf16[64,1,6]{2,1,0:T(2,128)(2,1)} %copy.122), calls=%async_computation.4 | async-start | bytes 65536 | tf_op jit(solution)/shard_map/all_to_all | solution.py:74
  27.2 3.7 copy.108
  31.4 20.6 %reduce.6 = bf16[3584,16]{1,0:T(8,128)(2,1)} reduce(bf16[3584,1,16]{2,1,0:T(2,128)(2,1)S(1)} %bitcast.85, bf16[]{:T(256)} %broadcast.80), dimensions={1}, to_apply=%bitcast.57.reduce_sub_computation | reduce | bytes 229378
  54.8 7.7 %all-to-all-start = ((bf16[8,2,3584]{2,1,0:T(2,128)(2,1)}), bf16[8,2,3584]{2,1,0:T(2,128)(2,1)S(1)}, u32[]{:S(2)}, u32[]{:S(2)}) async-start(bf16[8,2,3584]{2,1,0:T(2,128)(2,1)} %reshape.181), calls=%async_computation | async-start | bytes 229376 | tf_op jit(solution)/shard_map/all_to_all | solution.py:57
  65.0 20.6 %reduce.7 = bf16[3584,16]{1,0:T(8,128)(2,1)} reduce(bf16[3584,1,16]{2,1,0:T(2,128)(2,1)S(1)} %bitcast.90, bf16[]{:T(256)} %broadcast.80), dimensions={1}, to_apply=%bitcast.59.reduce_sub_computation | reduce | bytes 229378
  88.4 7.8 %all-to-all-start.1 = ((bf16[8,2,3584]{2,1,0:T(2,128)(2,1)}), bf16[8,2,3584]{2,1,0:T(2,128)(2,1)S(1)}, u32[]{:S(2)}, u32[]{:S(2)}) async-start(bf16[8,2,3584]{2,1,0:T(2,128)(2,1)} %reshape.183), calls=%async_computation.1 | async-start | bytes 229376 | tf_op jit(solution)/shard_map/all_to_all | solution.py:58
  98.7 20.6 %reduce.8 = bf16[3584,16]{1,0:T(8,128)(2,1)} reduce(bf16[3584,1,16]{2,1,0:T(2,128)(2,1)S(1)} %bitcast.86, bf16[]{:T(256)} %broadcast.80), dimensions={1}, to_apply=%bitcast.61.reduce_sub_computation | reduce | bytes 229378
  122.1 7.2 %all-to-all-start.2 = ((bf16[8,2,3584]{2,1,0:T(2,128)(2,1)}), bf16[8,2,3584]{2,1,0:T(2,128)(2,1)S(1)}, u32[]{:S(2)}, u32[]{:S(2)}) async-start(bf16[8,2,3584]{2,1,0:T(2,128)(2,1)} %reshape.185), calls=%async_computation.2 | async-start | bytes 229376 | tf_op jit(solution)/shard_map/all_to_all | solution.py:59
  129.6 5.3 all-to-all-done.2
  137.0 11.4 %all-to-all-start.3 = ((bf16[64,6,3584]{2,1,0:T(8,128)(2,1)}), bf16[64,6,3584]{2,1,0:T(8,128)(2,1)}, u32[]{:S(2)}, u32[]{:S(2)}) async-start(bf16[64,6,3584]{2,1,0:T(8,128)(2,1)} %bitcast.84), calls=%async_computation.3 | async-start | bytes 7340032 | tf_op jit(solution)/shard_map/all_to_all | solution.py:72
  148.7 83.3 %all-to-all-done.3 = bf16[64,6,3584]{2,1,0:T(8,128)(2,1)} async-done(((bf16[64,6,3584]{2,1,0:T(8,128)(2,1)}), bf16[64,6,3584]{2,1,0:T(8,128)(2,1)}, u32[]{:S(2)}, u32[]{:S(2)}) %all-to-all-start.3) | async-done | bytes 2752544 | tf_op jit(solution)/shard_map/all_to_all | solution.py:72
  234.1 7.4 %all-to-all-start.5 = ((bf16[64,6,3584]{2,1,0:T(8,128)(2,1)}), bf16[64,6,3584]{2,1,0:T(8,128)(2,1)}, u32[]{:S(2)}, u32[]{:S(2)}) async-start(bf16[64,6,3584]{2,1,0:T(8,128)(2,1)} %bitcast.83), calls=%async_computation.5 | async-start | bytes 7340032 | tf_op jit(solution)/shard_map/all_to_all | solution.py:73
  245.1 79.2 %all-to-all-done.5 = bf16[64,6,3584]{2,1,0:T(8,128)(2,1)} async-done(((bf16[64,6,3584]{2,1,0:T(8,128)(2,1)}), bf16[64,6,3584]{2,1,0:T(8,128)(2,1)}, u32[]{:S(2)}, u32[]{:S(2)}) %all-to-all-start.5) | async-done | bytes 2752544 | tf_op jit(solution)/shard_map/all_to_all | solution.py:73
  325.3 7.9 %all-to-all-start.6 = ((bf16[8,1,448,128]{3,2,1,0:T(8,128)(2,1)}), bf16[8,1,448,128]{3,2,1,0:T(8,128)(2,1)}, u32[]{:S(2)}, u32[]{:S(2)}) async-start(bf16[8,1,448,128]{3,2,1,0:T(8,128)(2,1)} %stack.5), calls=%async_computation.6 | async-start | bytes 1835008 | tf_op jit(solution)/shard_map/all_to_all | solution.py:65
  340.7 28.9 %all_gather.6 = bf16[1,3584,128]{2,1,0:T(8,128)(2,1)S(1)} all-gather(bf16[1,448,128]{2,1,0:T(8,128)(2,1)S(1)} %copy.130), channel_id=1, replica_groups=mesh['dp'=8,'expert'=64] {'dp'}, dimensions={1}, use_global_device_ids=true | all-gather | bytes 1032192 | tf_op jit(solution)/shard_map/all_gather | solution.py:63
  369.5 16.6 %all_gather.7 = bf16[1,3584,128]{2,1,0:T(8,128)(2,1)S(1)} all-gather(bf16[1,448,128]{2,1,0:T(8,128)(2,1)S(1)} %copy.129), channel_id=1, replica_groups=mesh['dp'=8,'expert'=64] {'dp'}, dimensions={1}, use_global_device_ids=true | all-gather | bytes 1032192 | tf_op jit(solution)/shard_map/all_gather | solution.py:62
  386.1 5.4 reshape.160
  391.6 5.5 reshape.163
  410.5 9.6 %all-to-all-start.8 = ((bf16[64,1,6]{2,1,0:T(2,128)(2,1)}), bf16[64,1,6]{2,1,0:T(2,128)(2,1)S(1)}, u32[]{:S(2)}, u32[]{:S(2)}) async-start(bf16[64,1,6]{2,1,0:T(2,128)(2,1)} %convert_element_type.149), calls=%async_computation.11 | async-start | bytes 65536 | tf_op jit(solution)/shard_map/all_to_all | solution.py:120
  420.1 5.0 fusion
  425.1 5.4 reshape.164
  430.6 10.8 %all-to-all-start.7 = ((bf16[64,6,3584]{2,1,0:T(8,128)(2,1)}), bf16[64,6,3584]{2,1,0:T(8,128)(2,1)}, u32[]{:S(2)}, u32[]{:S(2)}) async-start(bf16[64,6,3584]{2,1,0:T(8,128)(2,1)} %reshape.164), calls=%async_computation.10 | async-start | bytes 7340032 | tf_op jit(solution)/shard_map/all_to_all | solution.py:113
  452.4 44.4 %reduce-scatter.6.cloned.1.call-done = bf16[1,448,128]{2,1,0:T(8,128)(2,1)} async-done(((bf16[1,3584,128]{2,1,0:T(8,128)(2,1)}), bf16[1,448,128]{2,1,0:T(8,128)(2,1)}) %reduce-scatter.6.cloned.1.call-update) | async-done | bytes 114704 | tf_op jit(solution)/shard_map/reduce_scatter | solution.py:105
  498.4 41.5 %reduce-scatter.8.cloned.1.call-done = bf16[1,448,128]{2,1,0:T(8,128)(2,1)} async-done(((bf16[1,3584,128]{2,1,0:T(8,128)(2,1)}), bf16[1,448,128]{2,1,0:T(8,128)(2,1)}) %reduce-scatter.8.cloned.1.call-update) | async-done | bytes 114704 | tf_op jit(solution)/shard_map/reduce_scatter | solution.py:108
  (103 shorter events, 68.5 us)
Async XLA Ops:
  7.2 122.2 %copy-start = (bf16[128,3584]{1,0:T(8,128)(2,1)S(1)}, bf16[128,3584]{1,0:T(8,128)(2,1)}, u32[]{:S(2)}) copy-start(bf16[128,3584]{1,0:T(8,128)(2,1)} %param.7) | copy-start | bytes 2752516
  12.9 41.9 %all-to-all-start.4 = ((bf16[64,1,6]{2,1,0:T(2,128)(2,1)}), bf16[64,1,6]{2,1,0:T(2,128)(2,1)S(1)}, u32[]{:S(2)}, u32[]{:S(2)}) async-start(bf16[64,1,6]{2,1,0:T(2,128)(2,1)} %copy.122), calls=%async_computation.4 | async-start | bytes 65536 | tf_op jit(solution)/shard_map/all_to_all | solution.py:74
  27.2 35.4 %copy-start.6 = (bf16[1,3584,16]{1,2,0:T(8,128)(2,1)S(1)}, bf16[1,3584,16]{1,2,0:T(8,128)(2,1)}, u32[]{:S(2)}) copy-start(bf16[1,3584,16]{1,2,0:T(8,128)(2,1)} %param.12) | copy-start | bytes 344068
  54.8 33.6 %all-to-all-start = ((bf16[8,2,3584]{2,1,0:T(2,128)(2,1)}), bf16[8,2,3584]{2,1,0:T(2,128)(2,1)S(1)}, u32[]{:S(2)}, u32[]{:S(2)}) async-start(bf16[8,2,3584]{2,1,0:T(2,128)(2,1)} %reshape.181), calls=%async_computation | async-start | bytes 229376 | tf_op jit(solution)/shard_map/all_to_all | solution.py:57
  62.6 33.6 %copy-start.7 = (bf16[1,3584,16]{1,2,0:T(8,128)(2,1)S(1)}, bf16[1,3584,16]{1,2,0:T(8,128)(2,1)}, u32[]{:S(2)}) copy-start(bf16[1,3584,16]{1,2,0:T(8,128)(2,1)} %param.13) | copy-start | bytes 344068
  88.4 33.7 %all-to-all-start.1 = ((bf16[8,2,3584]{2,1,0:T(2,128)(2,1)}), bf16[8,2,3584]{2,1,0:T(2,128)(2,1)S(1)}, u32[]{:S(2)}, u32[]{:S(2)}) async-start(bf16[8,2,3584]{2,1,0:T(2,128)(2,1)} %reshape.183), calls=%async_computation.1 | async-start | bytes 229376 | tf_op jit(solution)/shard_map/all_to_all | solution.py:58
  122.1 12.8 %all-to-all-start.2 = ((bf16[8,2,3584]{2,1,0:T(2,128)(2,1)}), bf16[8,2,3584]{2,1,0:T(2,128)(2,1)S(1)}, u32[]{:S(2)}, u32[]{:S(2)}) async-start(bf16[8,2,3584]{2,1,0:T(2,128)(2,1)} %reshape.185), calls=%async_computation.2 | async-start | bytes 229376 | tf_op jit(solution)/shard_map/all_to_all | solution.py:59
  137.0 11.4 %copy-start.3 = (bf16[128,3584]{1,0:T(8,128)(2,1)S(1)}, bf16[128,3584]{1,0:T(8,128)(2,1)}, u32[]{:S(2)}) copy-start(bf16[128,3584]{1,0:T(8,128)(2,1)} %param.8) | copy-start | bytes 2752516
  137.0 95.0 %all-to-all-start.3 = ((bf16[64,6,3584]{2,1,0:T(8,128)(2,1)}), bf16[64,6,3584]{2,1,0:T(8,128)(2,1)}, u32[]{:S(2)}, u32[]{:S(2)}) async-start(bf16[64,6,3584]{2,1,0:T(8,128)(2,1)} %bitcast.84), calls=%async_computation.3 | async-start | bytes 7340032 | tf_op jit(solution)/shard_map/all_to_all | solution.py:72
  234.1 90.1 %all-to-all-start.5 = ((bf16[64,6,3584]{2,1,0:T(8,128)(2,1)}), bf16[64,6,3584]{2,1,0:T(8,128)(2,1)}, u32[]{:S(2)}, u32[]{:S(2)}) async-start(bf16[64,6,3584]{2,1,0:T(8,128)(2,1)} %bitcast.83), calls=%async_computation.5 | async-start | bytes 7340032 | tf_op jit(solution)/shard_map/all_to_all | solution.py:73
  325.3 75.5 %all-to-all-start.6 = ((bf16[8,1,448,128]{3,2,1,0:T(8,128)(2,1)}), bf16[8,1,448,128]{3,2,1,0:T(8,128)(2,1)}, u32[]{:S(2)}, u32[]{:S(2)}) async-start(bf16[8,1,448,128]{3,2,1,0:T(8,128)(2,1)} %stack.5), calls=%async_computation.6 | async-start | bytes 1835008 | tf_op jit(solution)/shard_map/all_to_all | solution.py:65
  333.3 117.5 %reduce-scatter.4.cloned.1.call-start = ((), (), s32[]{:S(2)}) async-start(), calls=%async_computation.12 | async-start | bytes 1032192 | tf_op jit(solution)/shard_map/reduce_scatter | solution.py:102
  337.1 32.4 %copy-start.4 = (bf16[1,448,128]{2,1,0:T(8,128)(2,1)}, bf16[1,448,128]{2,1,0:T(8,128)(2,1)S(1)}, u32[]{:S(2)}) copy-start(bf16[1,448,128]{2,1,0:T(8,128)(2,1)S(1)} %copy.129) | copy-start | bytes 344068
  340.7 50.9 %copy-start.5 = (bf16[1,448,128]{2,1,0:T(8,128)(2,1)}, bf16[1,448,128]{2,1,0:T(8,128)(2,1)S(1)}, u32[]{:S(2)}) copy-start(bf16[1,448,128]{2,1,0:T(8,128)(2,1)S(1)} %copy.130) | copy-start | bytes 344068
  397.1 2.9 copy-start.1
  400.9 3.7 copy-start.2
  410.5 20.0 %all-to-all-start.8 = ((bf16[64,1,6]{2,1,0:T(2,128)(2,1)}), bf16[64,1,6]{2,1,0:T(2,128)(2,1)S(1)}, u32[]{:S(2)}, u32[]{:S(2)}) async-start(bf16[64,1,6]{2,1,0:T(2,128)(2,1)} %convert_element_type.149), calls=%async_computation.11 | async-start | bytes 65536 | tf_op jit(solution)/shard_map/all_to_all | solution.py:120
  430.6 111.0 %all-to-all-start.7 = ((bf16[64,6,3584]{2,1,0:T(8,128)(2,1)}), bf16[64,6,3584]{2,1,0:T(8,128)(2,1)}, u32[]{:S(2)}, u32[]{:S(2)}) async-start(bf16[64,6,3584]{2,1,0:T(8,128)(2,1)} %reshape.164), calls=%async_computation.10 | async-start | bytes 7340032 | tf_op jit(solution)/shard_map/all_to_all | solution.py:113
  441.4 4.1 copy-start.8
  441.4 55.5 %reduce-scatter.6.cloned.1.call-start = ((), (), s32[]{:S(2)}) async-start(), calls=%async_computation.13 | async-start | bytes 1032192 | tf_op jit(solution)/shard_map/reduce_scatter | solution.py:105
  445.2 94.8 %reduce-scatter.8.cloned.1.call-start = ((), (), s32[]{:S(2)}) async-start(), calls=%async_computation.14 | async-start | bytes 1032192 | tf_op jit(solution)/shard_map/reduce_scatter | solution.py:108
Sparse Core Ops, SparseCore 0:
  409.9 40.5 reduce-scatter.3
  453.6 43.2 reduce-scatter.5
  499.7 40.2 reduce-scatter.7
